TPU v7x, 256 devices: a whole 4x4x8 slice. The times are simulated.
256 devices in a mesh: dp: 8 (over y, core), ctx: 32 (over z, x).
Axes of the slice: x: 4, y: 4, z: 8, core: 2. Of those that a mesh axis runs over, the one named last changes fastest.
Arguments:
- normed_hidden_input: bfloat16 [8, 4096, 4096], P('dp', 'ctx'), may hold values from -6 to 6
- frozen_query_projection: bfloat16 [8, 4096, 4096], P('dp', 'ctx'), may hold values from -24 to 24
- frozen_key_projection: bfloat16 [8, 4096, 4096], P('dp', 'ctx'), may hold values from -24 to 24
- frozen_value_projection: bfloat16 [8, 4096, 4096], P('dp', 'ctx'), may hold values from -6 to 6
- cotangent: bfloat16 [8, 4096, 4096], P('dp', 'ctx'), may hold values from -0.119628906 to 0.119628906
- adapter_down_maps: bfloat16 [3, 4096, 16], replicated, may hold values from -0.09375 to 0.09375
- adapter_up_maps: bfloat16 [3, 16, 4096], replicated, may hold values from -1.5 to 1.5
- head_shift_mask: int32 [32], replicated, may hold values from 0 to 1, as said below
Outputs:
- context: bfloat16 [8, 4096, 4096], P('dp', 'ctx')
- grad_down: float32 [3, 4096, 16], replicated
- grad_up: float32 [3, 16, 4096], replicated
Inputs may be any that keep to these rules, and one draw needn't show every extreme that they name: `head_shift_mask`: exactly half of the entries are 1, the rest 0; which heads are shifted varies.
All inputs are finite; a program needn't handle non-finite values.
Results may differ from a plain program's by a relative error of at most 0.02.
The roundings to bfloat16 on the way count: a program that leaves them out, or rounds other values in their place, can miss the bound.
Values may be sent and summed in bfloat16 or wider, within the bound.
A program may use at most 64 MiB of HBM per device.

v0:
```python
import math
import jax
import jax.numpy as jnp
from jax import lax
from jax.sharding import PartitionSpec as P

HEAD_DIM = 128
GROUP = 1024
SHIFT = 512
adapter_scale = 0.25


def shift_heads(values, shift_flags, amount):
    rolled = jnp.roll(values, amount, axis=0)
    return jnp.where(shift_flags[None, :, None] == 1, rolled, values)


def group_block(segment_list):
    queries, key_rows, value_rows, grad_out = segment_list
    group_len = queries.shape[0]
    softmax_scale = 1.0 / math.sqrt(queries.shape[2])
    scores = (
        jnp.einsum("qhe,khe->hqk", queries, key_rows, preferred_element_type=jnp.float32)
        * softmax_scale
    )
    row_ids = lax.broadcasted_iota(jnp.int32, (group_len, group_len), 0)
    col_ids = lax.broadcasted_iota(jnp.int32, (group_len, group_len), 1)
    scores = jnp.where((col_ids <= row_ids)[None], scores, -1e30)
    highest = jnp.max(scores, axis=2, keepdims=True)
    exponent = jnp.exp(scores - highest)
    weights = exponent / jnp.sum(exponent, axis=2, keepdims=True)
    weights_low = weights.astype(jnp.bfloat16)
    attended = jnp.einsum(
        "hqk,khe->qhe", weights_low, value_rows, preferred_element_type=jnp.float32
    ).astype(jnp.bfloat16)
    weight_grad = jnp.einsum(
        "qhe,khe->hqk", grad_out, value_rows, preferred_element_type=jnp.float32
    )
    row_inner = jnp.sum(grad_out.astype(jnp.float32) * attended.astype(jnp.float32), axis=2)
    score_grad = weights * (weight_grad - jnp.transpose(row_inner)[:, :, None])
    score_low = score_grad.astype(jnp.bfloat16)
    query_grad = (
        jnp.einsum("hqk,khe->qhe", score_low, key_rows, preferred_element_type=jnp.float32)
        * softmax_scale
    ).astype(jnp.bfloat16)
    key_grad = (
        jnp.einsum("hqk,qhe->khe", score_low, queries, preferred_element_type=jnp.float32)
        * softmax_scale
    ).astype(jnp.bfloat16)
    value_grad = jnp.einsum(
        "hqk,qhe->khe", weights_low, grad_out, preferred_element_type=jnp.float32
    ).astype(jnp.bfloat16)
    return (attended, query_grad, key_grad, value_grad)


def attend_heads(queries, key_rows, value_rows, grad_out, shift_flags):
    total, heads, depth = queries.shape
    groups = total // GROUP

    def regroup(array):
        return shift_heads(array, shift_flags, -SHIFT).reshape(groups, GROUP, heads, depth)

    results = lax.map(
        group_block, (regroup(queries), regroup(key_rows), regroup(value_rows), regroup(grad_out))
    )
    return tuple(
        (
            shift_heads(output_part.reshape(total, heads, depth), shift_flags, SHIFT)
            for output_part in results
        )
    )


def body(
    normed_hidden_input,
    frozen_query_projection,
    frozen_key_projection,
    frozen_value_projection,
    cotangent,
    adapter_down_maps,
    adapter_up_maps,
    head_shift_mask,
):
    ctx_count = lax.axis_size("ctx")
    model_width = normed_hidden_input.shape[2]
    local_width = model_width // ctx_count
    local_heads = local_width // HEAD_DIM
    hidden_rows = normed_hidden_input[0]
    reduced_rank_rows = jnp.einsum(
        "vl,hlq->hvq", hidden_rows, adapter_down_maps, preferred_element_type=jnp.float32
    ).astype(jnp.bfloat16)
    frozen_stack = jnp.stack(
        [frozen_query_projection[0], frozen_key_projection[0], frozen_value_projection[0]]
    )
    grad_heads = lax.all_to_all(cotangent[0], "ctx", split_axis=1, concat_axis=0, tiled=True)
    local_flags = lax.dynamic_slice_in_dim(
        head_shift_mask, lax.axis_index("ctx") * local_heads, local_heads
    )
    adapter_update = jnp.einsum(
        "bsc,bci->bsi", reduced_rank_rows, adapter_up_maps, preferred_element_type=jnp.float32
    )
    projected_sequence = (frozen_stack.astype(jnp.float32) + adapter_scale * adapter_update).astype(
        jnp.bfloat16
    )
    projected_rows = lax.all_to_all(
        projected_sequence, "ctx", split_axis=2, concat_axis=1, tiled=True
    )
    seq_total = projected_rows.shape[1]
    head_view = projected_rows.reshape(3, seq_total, local_heads, HEAD_DIM)
    grad_view = grad_heads.reshape(seq_total, local_heads, HEAD_DIM)
    attended, query_grad, key_grad, value_grad = attend_heads(
        head_view[0], head_view[1], head_view[2], grad_view, local_flags
    )
    context = lax.all_to_all(
        attended.reshape(seq_total, local_width), "ctx", split_axis=0, concat_axis=1, tiled=True
    )
    grad_stack = jnp.stack([query_grad, key_grad, value_grad]).reshape(3, seq_total, local_width)
    token_gradient = lax.all_to_all(grad_stack, "ctx", split_axis=1, concat_axis=2, tiled=True)
    up_contribution = adapter_scale * jnp.einsum(
        "xvq,xvh->xqh", reduced_rank_rows, token_gradient, preferred_element_type=jnp.float32
    )
    backward_rank_rows = jnp.einsum(
        "efu,eau->efa", token_gradient, adapter_up_maps, preferred_element_type=jnp.float32
    ).astype(jnp.bfloat16)
    down_contribution = adapter_scale * jnp.einsum(
        "ow,noi->nwi", hidden_rows, backward_rank_rows, preferred_element_type=jnp.float32
    )
    grad_down, grad_up = lax.psum((down_contribution, up_contribution), ("dp", "ctx"))
    return (context[None], grad_down, grad_up)


def solution(mesh):
    placed = (
        P("dp", "ctx", None),
        P("dp", "ctx", None),
        P("dp", "ctx", None),
        P("dp", "ctx", None),
        P("dp", "ctx", None),
        P(),
        P(),
        P(),
    )
    return jax.shard_map(
        body,
        mesh=mesh,
        in_specs=placed,
        out_specs=(P("dp", "ctx", None), P(), P()),
        check_vma=False,
    )
```

profile of v0, /device:TPU:2, one launch (start us, length us, event | category | flops | bytes accessed | tf_op | source)
XLA Modules:
  0.0 671.0 jit_solution(5635035876560614335)
XLA Ops:
  7.2 2.4 copy.90
  9.6 11.6 %all-to-all-start.1 = ((bf16[128,32,128]{0,2,1:T(8,128)(2,1)}), bf16[128,32,128]{0,2,1:T(8,128)(2,1)S(1)}, u32[]{:S(2)}, u32[]{:S(2)}) async-start(bf16[128,32,128]{0,2,1:T(8,128)(2,1)} %bitcast.39), calls=%async_computation.1 | async-start | bytes 2097152 | tf_op jit(solution)/shard_map/all_to_all | solution.py:95
  22.3 3.7 add_convert_fusion
  26.1 7.1 %copy.79 = bf16[3,128,4096]{1,0,2:T(4,128)(2,1)} copy(bf16[3,128,4096]{2,1,0:T(8,128)(2,1)} %add_convert_fusion) | data formatting | bytes 6291456 | tf_op jit(solution)/shard_map/convert_element_type | solution.py:102
  33.2 16.1 %all-to-all-done.1 = bf16[128,32,128]{0,2,1:T(8,128)(2,1)S(1)} async-done(((bf16[128,32,128]{0,2,1:T(8,128)(2,1)}), bf16[128,32,128]{0,2,1:T(8,128)(2,1)S(1)}, u32[]{:S(2)}, u32[]{:S(2)}) %all-to-all-start.1) | async-done | bytes 1048608 | tf_op jit(solution)/shard_map/all_to_all | solution.py:95
  49.3 5.6 all-to-all-start
  58.0 1.6 copy.91
  59.8 1.2 broadcast_select_fusion
  61.0 85.8 %all-to-all-done = bf16[3,128,4096]{1,0,2:T(4,128)(2,1)} async-done(((bf16[3,128,4096]{1,0,2:T(4,128)(2,1)}), bf16[3,128,4096]{1,0,2:T(4,128)(2,1)}, u32[]{:S(2)}, u32[]{:S(2)}) %all-to-all-start) | async-done | bytes 3145760 | tf_op jit(solution)/shard_map/all_to_all | solution.py:105
  146.8 2.6 copy.80
  149.5 1.6 fusion.47
  151.7 1.7 fusion.46
  153.4 1.3 copy.87
  155.4 2.2 copy.84
  157.8 1.6 copy.86
  159.4 2.3 copy.81
  162.7 2.3 copy.83
  165.0 1.3 pad_maximum_fusion.2
  166.3 1.1 select_bitcast_fusion
  170.1 81.5 %while.16 = (s32[]{:T(128)}, bf16[4,1024,1,128]{3,1,0,2:T(8,128)(2,1)}, bf16[4,1024,1,128]{3,1,0,2:T(8,128)(2,1)}, bf16[4,1024,1,128]{3,1,0,2:T(8,128)(2,1)}, bf...) while((s32[]{:T(128)}, ...), condition=%wide.region_4.5_spmd, body=%wide.region_0.4_spmd.sunk | while | flops 1642329088 | bytes 69517472 | solution.py:63
  170.1 1.7 fusion.78
  172.3 1.2 constant_dynamic-slice_fusion.2
  175.7 3.9 fusion.80
  179.6 1.9 multiply_convert_fusion.2
  181.5 2.5 fusion.83
  185.1 1.8 constant_dynamic-update-slice_fusion.7
  186.9 1.4 fusion.81
  190.4 1.7 fusion.78
  192.7 1.2 constant_dynamic-slice_fusion.2
  196.0 3.9 fusion.80
  199.9 1.9 multiply_convert_fusion.2
  201.8 2.5 fusion.83
  205.4 1.8 constant_dynamic-update-slice_fusion.7
  207.2 1.4 fusion.81
  208.8 1.1 copy.141
  210.8 1.7 fusion.78
  213.0 1.2 constant_dynamic-slice_fusion.2
  216.4 3.9 fusion.80
  220.3 1.9 multiply_convert_fusion.2
  222.2 2.5 fusion.83
  225.8 1.8 constant_dynamic-update-slice_fusion.7
  227.6 1.4 fusion.81
  231.1 1.7 fusion.78
  233.4 1.2 constant_dynamic-slice_fusion.2
  236.8 3.9 fusion.80
  240.6 1.9 multiply_convert_fusion.2
  242.5 2.5 fusion.83
  246.2 1.8 constant_dynamic-update-slice_fusion.7
  248.0 1.4 fusion.81
  251.5 1.3 slice_bitcast_fusion.1
  253.9 1.2 slice_bitcast_fusion.2
  257.6 20.8 %copy.107 = bf16[3,4096,128]{2,0,1:T(4,128)(2,1)} copy(bf16[3,4096,128]{2,1,0:T(8,128)(2,1)S(1)} %maximum_bitcast_fusion) | data formatting | bytes 6291456 | tf_op jit(solution)/shard_map/reshape | solution.py:117
  278.4 8.5 %all-to-all-start.3 = ((bf16[3,4096,128]{2,0,1:T(4,128)(2,1)}), bf16[3,4096,128]{2,0,1:T(4,128)(2,1)}, u32[]{:S(2)}, u32[]{:S(2)}) async-start(bf16[3,4096,128]{2,0,1:T(4,128)(2,1)} %copy.107), calls=%async_computation.3 | async-start | bytes 8388608 | tf_op jit(solution)/shard_map/all_to_all | solution.py:118
  288.2 91.0 %all-to-all-done.3 = bf16[3,4096,128]{2,0,1:T(4,128)(2,1)} async-done(((bf16[3,4096,128]{2,0,1:T(4,128)(2,1)}), bf16[3,4096,128]{2,0,1:T(4,128)(2,1)}, u32[]{:S(2)}, u32[]{:S(2)}) %all-to-all-start.3) | async-done | bytes 3145760 | tf_op jit(solution)/shard_map/all_to_all | solution.py:118
  379.1 7.5 %all-to-all-start.2 = ((bf16[32,128,128]{2,1,0:T(8,128)(2,1)}), bf16[32,128,128]{2,1,0:T(8,128)(2,1)S(1)}, u32[]{:S(2)}, u32[]{:S(2)}) async-start(bf16[32,128,128]{2,1,0:T(8,128)(2,1)} %broadcast_select_fusion.1), calls=%async_computation.2 | async-start | bytes 2097152 | tf_op jit(solution)/shard_map/all_to_all | solution.py:114
  386.7 2.7 copy.108
  389.4 1.6 copy-done.3
  391.0 1.4 convolution_multiply_fusion.2
  392.4 4.2 fusion.33
  396.7 16.3 %all-to-all-done.2 = bf16[32,128,128]{2,1,0:T(8,128)(2,1)S(1)} async-done(((bf16[32,128,128]{2,1,0:T(8,128)(2,1)}), bf16[32,128,128]{2,1,0:T(8,128)(2,1)S(1)}, u32[]{:S(2)}, u32[]{:S(2)}) %all-to-all-start.2) | async-done | bytes 1048608 | tf_op jit(solution)/shard_map/all_to_all | solution.py:114
  413.6 1.3 copy.110
  414.9 245.1 %all-reduce.3.cloned.1.call-done = (f32[3,4096,16]{1,2,0:T(8,128)}, f32[3,16,4096]{2,1,0:T(8,128)}) async-done(((f32[3,4096,16]{1,2,0:T(8,128)}, f32[3,16,4096]{2,1,0:T(8,128)}), (f32[3,4096,16]{1,2,0:T(8,128)}, f32[3,16,4096]{2,1,0:T(8,128)})) %all-reduce.3.cloned.1.call-update) | async-done | bytes 1572880 | tf_op jit(solution)/shard_map/psum | solution.py:128
  660.1 2.1 copy.167
  662.1 2.1 copy.168
  (110 shorter events, 36.8 us)
Async XLA Ops:
  7.2 14.1 %copy-start = (bf16[1,128,4096]{2,1,0:T(8,128)(2,1)S(1)}, bf16[1,128,4096]{2,1,0:T(8,128)(2,1)}, u32[]{:S(2)}) copy-start(bf16[1,128,4096]{2,1,0:T(8,128)(2,1)} %param.10) | copy-start | bytes 3145732
  7.2 14.0 %copy-start.11 = (bf16[3,4096,16]{1,2,0:T(8,128)(2,1)S(1)}, bf16[3,4096,16]{1,2,0:T(8,128)(2,1)}, u32[]{:S(2)}) copy-start(bf16[3,4096,16]{1,2,0:T(8,128)(2,1)} %param.15) | copy-start | bytes 1179652
  7.2 15.1 %copy-start.12 = (bf16[3,16,4096]{2,1,0:T(8,128)(2,1)S(1)}, bf16[3,16,4096]{2,1,0:T(8,128)(2,1)}, u32[]{:S(2)}) copy-start(bf16[3,16,4096]{2,1,0:T(8,128)(2,1)} %param.16) | copy-start | bytes 1179652
  9.6 39.7 %all-to-all-start.1 = ((bf16[128,32,128]{0,2,1:T(8,128)(2,1)}), bf16[128,32,128]{0,2,1:T(8,128)(2,1)S(1)}, u32[]{:S(2)}, u32[]{:S(2)}) async-start(bf16[128,32,128]{0,2,1:T(8,128)(2,1)} %bitcast.39), calls=%async_computation.1 | async-start | bytes 2097152 | tf_op jit(solution)/shard_map/all_to_all | solution.py:95
  21.7 0.6 copy-start.14
  33.2 21.8 %copy-start.16 = (s32[32]{0:T(128)S(1)}, s32[32]{0:T(128)}, u32[]{:S(2)}) copy-start(s32[32]{0:T(128)} %param.17) | copy-start | bytes 388
  49.3 97.5 %all-to-all-start = ((bf16[3,128,4096]{1,0,2:T(4,128)(2,1)}), bf16[3,128,4096]{1,0,2:T(4,128)(2,1)}, u32[]{:S(2)}, u32[]{:S(2)}) async-start(bf16[3,128,4096]{1,0,2:T(4,128)(2,1)} %copy.79), calls=%async_computation | async-start | bytes 8388608 | tf_op jit(solution)/shard_map/all_to_all | solution.py:105
  165.0 2.5 copy-start.9
  166.3 2.3 copy-start.10
  167.5 1.5 copy-start.8
  171.8 2.0 copy-start.1
  175.7 3.9 copy-start.2
  192.2 2.0 copy-start.1
  196.0 3.9 copy-start.2
  212.5 2.0 copy-start.1
  216.4 3.9 copy-start.2
  232.9 2.0 copy-start.1
  236.7 3.9 copy-start.2
  251.5 4.6 copy-start.7
  252.9 3.7 copy-start.4
  252.9 3.7 copy-start.5
  278.4 8.5 %copy-start.6 = (bf16[4,1024,1,128]{3,1,0,2:T(8,128)(2,1)S(1)}, bf16[4,1024,1,128]{3,1,0,2:T(8,128)(2,1)}, u32[]{:S(2)}) copy-start(bf16[4,1024,1,128]{3,1,0,2:T(8,128)(2,1)} %get-tuple-element.53) | copy-start | bytes 3145732
  278.4 100.7 %all-to-all-start.3 = ((bf16[3,4096,128]{2,0,1:T(4,128)(2,1)}), bf16[3,4096,128]{2,0,1:T(4,128)(2,1)}, u32[]{:S(2)}, u32[]{:S(2)}) async-start(bf16[3,4096,128]{2,0,1:T(4,128)(2,1)} %copy.107), calls=%async_computation.3 | async-start | bytes 8388608 | tf_op jit(solution)/shard_map/all_to_all | solution.py:118
  379.1 33.8 %all-to-all-start.2 = ((bf16[32,128,128]{2,1,0:T(8,128)(2,1)}), bf16[32,128,128]{2,1,0:T(8,128)(2,1)S(1)}, u32[]{:S(2)}, u32[]{:S(2)}) async-start(bf16[32,128,128]{2,1,0:T(8,128)(2,1)} %broadcast_select_fusion.1), calls=%async_computation.2 | async-start | bytes 2097152 | tf_op jit(solution)/shard_map/all_to_all | solution.py:114
  386.6 4.4 copy-start.15
  386.6 5.8 copy-start.13
  386.7 273.4 %all-reduce.3.cloned.1.call-start = ((), (), s32[]{:S(2)}) async-start(), calls=%async_computation.4 | async-start | bytes 3145728 | tf_op jit(solution)/shard_map/psum | solution.py:128
  389.4 1.6 copy-start.3
Sparse Core Ops, SparseCore 0:
  396.8 263.2 all-reduce.2
where the time goes:
time: 673 us; the launch traced here: 671 us
  waiting for transfers between devices  454 us (67%)
  local copies, waits for them, and re-layouts  98.2 us (15%)
  matrix products  59.2 us (9%)
  starting transfers between devices  33.3 us (5%)
  between operations  15.1 us (2%)
  other arithmetic  10.7 us (2%)
    psum x1, waiting for transfers between devices, body(): lax.psum((down_contribution, up_contribution), ('dp', 'ctx'))  245 us
    all_to_all x1, waiting for transfers between devices, body(): lax.all_to_all(grad_stack, 'ctx', split_axis=1, concat_axis=2, tiled=True)  91 us
    all_to_all x1, waiting for transfers between devices, body(): lax.all_to_all(projected_sequence, 'ctx', split_axis=2, concat_axis=1, ti...  85.8 us
    dynamic_update_slice x24, local copies, waits for them, and re-layouts, attend_heads(): lax.map(group_block, (regroup(queries), regroup(key_rows), regroup(value_...  23.5 us
    reshape x1, local copies, waits for them, and re-layouts, body(): jnp.stack([query_grad, key_grad, value_grad])  20.8 us
    all_to_all x1, waiting for transfers between devices, body(): lax.all_to_all(attended.reshape(seq_total, local_width), 'ctx', split_axi...  16.3 us
    all_to_all x1, waiting for transfers between devices, body(): lax.all_to_all(cotangent[0], 'ctx', split_axis=1, concat_axis=0, tiled=True)  16.1 us
    dot_general x4, matrix products, group_block(): jnp.einsum('hqk,khe->qhe', weights_low, value_rows, preferred_element_typ...  15.5 us
  transfers between devices with their start and end apart: 5, of which 5 were waited for; matrix products, arithmetic and copies ran while one was open for 4% of the time, Pallas kernels for 0%

commit v1 on v0

--- a/solution.py
+++ b/solution.py
@@ -1,3 +1,4 @@
+import functools
 import math
 import jax
 import jax.numpy as jnp
@@ -8,6 +9,21 @@
 GROUP = 1024
 SHIFT = 512
 adapter_scale = 0.25
+
+
+def register_the_region(vals, dev_axis):
+    return jnp.concatenate(
+        jax.lax.all_to_all(
+            jnp.stack(jnp.split(vals, jax.lax.psum(1, dev_axis), 0), 0),
+            dev_axis,
+            split_axis=0,
+            concat_axis=0,
+        ),
+        1,
+    )
+
+
+show_side = functools.partial(register_the_region, dev_axis="ctx")
 
 
 def shift_heads(values, shift_flags, amount):
@@ -111,9 +127,7 @@
     attended, query_grad, key_grad, value_grad = attend_heads(
         head_view[0], head_view[1], head_view[2], grad_view, local_flags
     )
-    context = lax.all_to_all(
-        attended.reshape(seq_total, local_width), "ctx", split_axis=0, concat_axis=1, tiled=True
-    )
+    context = show_side(attended.reshape(seq_total, local_width))
     grad_stack = jnp.stack([query_grad, key_grad, value_grad]).reshape(3, seq_total, local_width)
     token_gradient = lax.all_to_all(grad_stack, "ctx", split_axis=1, concat_axis=2, tiled=True)
     up_contribution = adapter_scale * jnp.einsum(

time: 673 us -> 673 us (level)
  local copies, waits for them, and re-layouts: 98.2 us -> 118 us
  waiting for transfers between devices: 454 us -> 435 us
    unnamed x34 -> x65, local copies, waits for them, and re-layouts: 10.3 us -> 29.5 us
    all_to_all x1, waiting for transfers between devices: 91 us -> 72.1 us  [body(): lax.all_to_all(grad_stack, 'ctx', split_axis=1, concat_axis=2, tiled=True)]
  transfers between devices with their start and end apart: 5 -> 5, of which waited for: 5 -> 5; matrix products, arithmetic and copies ran while one was open for 4% -> 7% of each run, Pallas kernels for 0% -> 0%
where the time goes in v1:
time: 673 us; the launch traced here: 671 us
  waiting for transfers between devices  435 us (65%)
  local copies, waits for them, and re-layouts  118 us (18%)
  matrix products  59.2 us (9%)
  starting transfers between devices  33.1 us (5%)
  between operations  15.1 us (2%)
  other arithmetic  9.89 us (1%)
    psum x1, waiting for transfers between devices, body(): lax.psum((down_contribution, up_contribution), ('dp', 'ctx'))  245 us
    all_to_all x1, waiting for transfers between devices, body(): lax.all_to_all(projected_sequence, 'ctx', split_axis=2, concat_axis=1, ti...  85.8 us
    all_to_all x1, waiting for transfers between devices, body(): lax.all_to_all(grad_stack, 'ctx', split_axis=1, concat_axis=2, tiled=True)  72.1 us
    unnamed x65, local copies, waits for them, and re-layouts  29.5 us
    dynamic_update_slice x24, local copies, waits for them, and re-layouts, attend_heads(): lax.map(group_block, (regroup(queries), regroup(key_rows), regroup(value_...  23.5 us
    reshape x1, local copies, waits for them, and re-layouts, body(): jnp.stack([query_grad, key_grad, value_grad])  20.8 us
    all_to_all x1, waiting for transfers between devices, register_the_region(): jax.lax.all_to_all(jnp.stack(jnp.split(vals, jax.lax.psum(1, dev_axis), 0...  16.3 us
    all_to_all x1, waiting for transfers between devices, body(): lax.all_to_all(cotangent[0], 'ctx', split_axis=1, concat_axis=0, tiled=True)  16.1 us
  transfers between devices with their start and end apart: 5, of which 5 were waited for; matrix products, arithmetic and copies ran while one was open for 7% of the time, Pallas kernels for 0%

profile of v1, /device:TPU:2, one launch (start us, length us, event | category | flops | bytes accessed | tf_op | source)
XLA Modules:
  0.0 671.1 jit_solution(4737546883255023125)
XLA Ops:
  7.2 2.4 copy.117
  9.6 11.6 %all-to-all-start.1 = ((bf16[128,32,128]{0,2,1:T(8,128)(2,1)}), bf16[128,32,128]{0,2,1:T(8,128)(2,1)S(1)}, u32[]{:S(2)}, u32[]{:S(2)}) async-start(bf16[128,32,128]{0,2,1:T(8,128)(2,1)} %bitcast.39), calls=%async_computation.1 | async-start | bytes 2097152 | tf_op jit(solution)/shard_map/all_to_all | solution.py:111
  22.3 3.7 add_convert_fusion
  26.1 7.1 %copy.106 = bf16[3,128,4096]{1,0,2:T(4,128)(2,1)} copy(bf16[3,128,4096]{2,1,0:T(8,128)(2,1)} %add_convert_fusion) | data formatting | bytes 6291456 | tf_op jit(solution)/shard_map/convert_element_type | solution.py:118
  33.2 16.1 %all-to-all-done.1 = bf16[128,32,128]{0,2,1:T(8,128)(2,1)S(1)} async-done(((bf16[128,32,128]{0,2,1:T(8,128)(2,1)}), bf16[128,32,128]{0,2,1:T(8,128)(2,1)S(1)}, u32[]{:S(2)}, u32[]{:S(2)}) %all-to-all-start.1) | async-done | bytes 1048608 | tf_op jit(solution)/shard_map/all_to_all | solution.py:111
  49.3 5.6 all-to-all-start
  58.0 1.6 copy.118
  59.8 1.2 broadcast_select_fusion
  61.0 85.8 %all-to-all-done = bf16[3,128,4096]{1,0,2:T(4,128)(2,1)} async-done(((bf16[3,128,4096]{1,0,2:T(4,128)(2,1)}), bf16[3,128,4096]{1,0,2:T(4,128)(2,1)}, u32[]{:S(2)}, u32[]{:S(2)}) %all-to-all-start) | async-done | bytes 3145760 | tf_op jit(solution)/shard_map/all_to_all | solution.py:121
  146.8 2.6 copy.107
  149.5 1.6 fusion.47
  151.7 1.7 fusion.46
  153.4 1.3 copy.114
  155.4 2.2 copy.111
  157.8 1.6 copy.113
  159.4 2.3 copy.108
  162.7 2.3 copy.110
  165.0 1.3 pad_maximum_fusion.2
  166.3 1.1 select_bitcast_fusion
  170.1 81.5 %while.16 = (s32[]{:T(128)}, bf16[4,1024,1,128]{3,1,0,2:T(8,128)(2,1)}, bf16[4,1024,1,128]{3,1,0,2:T(8,128)(2,1)}, bf16[4,1024,1,128]{3,1,0,2:T(8,128)(2,1)}, bf...) while((s32[]{:T(128)}, ...), condition=%wide.region_4.5_spmd, body=%wide.region_0.4_spmd.sunk | while | flops 1642329088 | bytes 69517472 | solution.py:79
  170.1 1.7 fusion.78
  172.3 1.2 constant_dynamic-slice_fusion.2
  175.7 3.9 fusion.80
  179.6 1.9 multiply_convert_fusion.2
  181.5 2.5 fusion.83
  185.1 1.8 constant_dynamic-update-slice_fusion.39
  186.9 1.4 fusion.81
  190.4 1.7 fusion.78
  192.7 1.2 constant_dynamic-slice_fusion.2
  196.0 3.9 fusion.80
  199.9 1.9 multiply_convert_fusion.2
  201.8 2.5 fusion.83
  205.4 1.8 constant_dynamic-update-slice_fusion.39
  207.2 1.4 fusion.81
  208.8 1.1 copy.167
  210.8 1.7 fusion.78
  213.0 1.2 constant_dynamic-slice_fusion.2
  216.4 3.9 fusion.80
  220.3 1.9 multiply_convert_fusion.2
  222.2 2.5 fusion.83
  225.8 1.8 constant_dynamic-update-slice_fusion.39
  227.6 1.4 fusion.81
  231.1 1.7 fusion.78
  233.4 1.2 constant_dynamic-slice_fusion.2
  236.8 3.9 fusion.80
  240.6 1.9 multiply_convert_fusion.2
  242.5 2.5 fusion.83
  246.2 1.8 constant_dynamic-update-slice_fusion.39
  248.0 1.4 fusion.81
  251.5 1.4 slice_bitcast_fusion.1
  253.8 1.2 slice_bitcast_fusion.2
  257.8 20.8 %copy.133 = bf16[3,4096,128]{2,0,1:T(4,128)(2,1)} copy(bf16[3,4096,128]{2,1,0:T(8,128)(2,1)S(1)} %maximum_bitcast_fusion) | data formatting | bytes 6291456 | tf_op jit(solution)/shard_map/reshape | solution.py:131
  278.5 8.4 %all-to-all-start.3 = ((bf16[3,4096,128]{2,0,1:T(4,128)(2,1)}), bf16[3,4096,128]{2,0,1:T(4,128)(2,1)}, u32[]{:S(2)}, u32[]{:S(2)}) async-start(bf16[3,4096,128]{2,0,1:T(4,128)(2,1)} %copy.133), calls=%async_computation.3 | async-start | bytes 8388608 | tf_op jit(solution)/shard_map/all_to_all | solution.py:132
  307.0 72.1 %all-to-all-done.3 = bf16[3,4096,128]{2,0,1:T(4,128)(2,1)} async-done(((bf16[3,4096,128]{2,0,1:T(4,128)(2,1)}), bf16[3,4096,128]{2,0,1:T(4,128)(2,1)}, u32[]{:S(2)}, u32[]{:S(2)}) %all-to-all-start.3) | async-done | bytes 3145760 | tf_op jit(solution)/shard_map/all_to_all | solution.py:132
  379.2 7.5 %all-to-all-start.2 = ((bf16[32,128,128]{2,1,0:T(8,128)(2,1)}), bf16[32,128,128]{2,1,0:T(8,128)(2,1)S(1)}, u32[]{:S(2)}, u32[]{:S(2)}) async-start(bf16[32,128,128]{2,1,0:T(8,128)(2,1)} %constant_dynamic-update-slice_fusion.4), calls=%async_computation.2 | async-start | bytes 2097152 | tf_op jit(solution)/shard_map/all_to_all | solution.py:16
  386.7 2.7 copy.134
  389.4 1.6 copy-done.3
  391.1 1.4 convolution_multiply_fusion.2
  392.5 4.2 fusion.33
  396.7 16.3 %all-to-all-done.2 = bf16[32,128,128]{2,1,0:T(8,128)(2,1)S(1)} async-done(((bf16[32,128,128]{2,1,0:T(8,128)(2,1)}), bf16[32,128,128]{2,1,0:T(8,128)(2,1)S(1)}, u32[]{:S(2)}, u32[]{:S(2)}) %all-to-all-start.2) | async-done | bytes 1048608 | tf_op jit(solution)/shard_map/all_to_all | solution.py:16
  413.6 1.3 copy.136
  415.0 245.1 %all-reduce.3.cloned.1.call-done = (f32[3,4096,16]{1,2,0:T(8,128)}, f32[3,16,4096]{2,1,0:T(8,128)}) async-done(((f32[3,4096,16]{1,2,0:T(8,128)}, f32[3,16,4096]{2,1,0:T(8,128)}), (f32[3,4096,16]{1,2,0:T(8,128)}, f32[3,16,4096]{2,1,0:T(8,128)})) %all-reduce.3.cloned.1.call-update) | async-done | bytes 1572880 | tf_op jit(solution)/shard_map/psum | solution.py:142
  660.1 2.1 copy.224
  662.2 2.1 copy.225
  (141 shorter events, 55.7 us)
Async XLA Ops:
  7.2 14.1 %copy-start = (bf16[1,128,4096]{2,1,0:T(8,128)(2,1)S(1)}, bf16[1,128,4096]{2,1,0:T(8,128)(2,1)}, u32[]{:S(2)}) copy-start(bf16[1,128,4096]{2,1,0:T(8,128)(2,1)} %param.10) | copy-start | bytes 3145732
  7.2 14.0 %copy-start.11 = (bf16[3,4096,16]{1,2,0:T(8,128)(2,1)S(1)}, bf16[3,4096,16]{1,2,0:T(8,128)(2,1)}, u32[]{:S(2)}) copy-start(bf16[3,4096,16]{1,2,0:T(8,128)(2,1)} %param.15) | copy-start | bytes 1179652
  7.2 15.1 %copy-start.12 = (bf16[3,16,4096]{2,1,0:T(8,128)(2,1)S(1)}, bf16[3,16,4096]{2,1,0:T(8,128)(2,1)}, u32[]{:S(2)}) copy-start(bf16[3,16,4096]{2,1,0:T(8,128)(2,1)} %param.16) | copy-start | bytes 1179652
  9.6 39.7 %all-to-all-start.1 = ((bf16[128,32,128]{0,2,1:T(8,128)(2,1)}), bf16[128,32,128]{0,2,1:T(8,128)(2,1)S(1)}, u32[]{:S(2)}, u32[]{:S(2)}) async-start(bf16[128,32,128]{0,2,1:T(8,128)(2,1)} %bitcast.39), calls=%async_computation.1 | async-start | bytes 2097152 | tf_op jit(solution)/shard_map/all_to_all | solution.py:111
  21.7 0.6 copy-start.14
  33.2 21.8 %copy-start.16 = (s32[32]{0:T(128)S(1)}, s32[32]{0:T(128)}, u32[]{:S(2)}) copy-start(s32[32]{0:T(128)} %param.17) | copy-start | bytes 388
  49.3 97.5 %all-to-all-start = ((bf16[3,128,4096]{1,0,2:T(4,128)(2,1)}), bf16[3,128,4096]{1,0,2:T(4,128)(2,1)}, u32[]{:S(2)}, u32[]{:S(2)}) async-start(bf16[3,128,4096]{1,0,2:T(4,128)(2,1)} %copy.106), calls=%async_computation | async-start | bytes 8388608 | tf_op jit(solution)/shard_map/all_to_all | solution.py:121
  165.0 2.5 copy-start.9
  166.3 2.3 copy-start.10
  167.5 1.5 copy-start.8
  171.8 2.0 copy-start.1
  175.7 3.9 copy-start.2
  192.2 2.0 copy-start.1
  196.0 3.9 copy-start.2
  212.5 2.0 copy-start.1
  216.4 3.9 copy-start.2
  232.9 2.0 copy-start.1
  236.7 3.9 copy-start.2
  251.5 4.6 copy-start.7
  251.5 4.7 copy-start.6
  255.1 1.6 copy-start.4
  255.1 1.6 copy-start.5
  278.5 100.6 %all-to-all-start.3 = ((bf16[3,4096,128]{2,0,1:T(4,128)(2,1)}), bf16[3,4096,128]{2,0,1:T(4,128)(2,1)}, u32[]{:S(2)}, u32[]{:S(2)}) async-start(bf16[3,4096,128]{2,0,1:T(4,128)(2,1)} %copy.133), calls=%async_computation.3 | async-start | bytes 8388608 | tf_op jit(solution)/shard_map/all_to_all | solution.py:132
  379.2 33.8 %all-to-all-start.2 = ((bf16[32,128,128]{2,1,0:T(8,128)(2,1)}), bf16[32,128,128]{2,1,0:T(8,128)(2,1)S(1)}, u32[]{:S(2)}, u32[]{:S(2)}) async-start(bf16[32,128,128]{2,1,0:T(8,128)(2,1)} %constant_dynamic-update-slice_fusion.4), calls=%async_computation.2 | async-start | bytes 2097152 | tf_op jit(solution)/shard_map/all_to_all | solution.py:16
  386.7 4.4 copy-start.15
  386.7 5.8 copy-start.13
  386.7 273.4 %all-reduce.3.cloned.1.call-start = ((), (), s32[]{:S(2)}) async-start(), calls=%async_computation.4 | async-start | bytes 3145728 | tf_op jit(solution)/shard_map/psum | solution.py:142
  389.4 1.6 copy-start.3
Sparse Core Ops, SparseCore 0:
  396.8 263.2 all-reduce.2
